TPU v7x, 32 devices: a whole 2x2x4 slice. The times are simulated.
32 devices in a mesh: ctx: 4 (over z), head: 8 (over y, x, core).
Axes of the slice: x: 2, y: 2, z: 4, core: 2. Of those that a mesh axis runs over, the one named last changes fastest.
Arguments:
- hidden: float32 [1024, 2304], P(('ctx', 'head')), may hold values from -40 to 40
- w_query: float32 [2304, 1536], P(None, 'head'), may hold values from -0.125 to 0.125
- w_down: float32 [2304, 576], replicated, may hold values from -0.125 to 0.125
- latent_gain: float32 [512], replicated, may hold values from 0.25 to 1.75
- w_key_up: float32 [512, 1024], P(None, 'head'), may hold values from -0.25 to 0.25
- w_value_up: float32 [512, 1024], P(None, 'head'), may hold values from -0.25 to 0.25
- w_out: float32 [1024, 2304], P('head'), may hold values from -0.1875 to 0.1875
Outputs:
- output: float32 [1024, 2304], P(('ctx', 'head'))
All inputs are finite; a program needn't handle non-finite values.
Results may differ from a plain program's by a relative error of at most 0.0003.
Values sent between devices are 32-bit elements; how exact they have to be, the bound alone decides.
A program may use at most 64 MiB of HBM per device.

v0:
```python
import jax
import jax.numpy as jnp
from jax import lax
from jax.sharding import PartitionSpec as P

EXACT = lax.Precision.HIGHEST
EPSILON = 1e-06
FLOOR = -1e30


def matmul(left, right):
    return jnp.dot(left, right, precision=EXACT, preferred_element_type=jnp.float32)


def on_device(hidden, w_query, w_down, latent_gain, w_key_up, w_value_up, w_out):
    rank = w_key_up.shape[0]
    nope = w_key_up.shape[1]
    down_part = matmul(hidden, w_down)
    raw_latent = down_part[:, :rank]
    meansq = jnp.mean(raw_latent * raw_latent, axis=-1, keepdims=True)
    own_latent = jnp.concatenate(
        [raw_latent * lax.rsqrt(meansq + EPSILON) * latent_gain, down_part[:, rank:]], axis=1
    )
    latent_block = lax.all_gather(own_latent, "head", axis=0, tiled=True)
    queries = matmul(lax.all_gather(hidden, "head", axis=0, tiled=True), w_query)
    row_count = queries.shape[0]
    score_scale = queries.shape[1] ** (-0.5)
    query_pos = lax.axis_index("ctx") * row_count + jnp.arange(row_count, dtype=jnp.int32)
    latent_part = latent_block[:, :rank]
    projected = jnp.concatenate(
        [matmul(latent_part, w_key_up), latent_block[:, rank:], matmul(latent_part, w_value_up)],
        axis=1,
    )
    shared_end = nope + latent_block.shape[1] - rank
    portion = lax.all_gather(projected, "ctx", axis=0, tiled=True)
    key_own = portion[:, :nope]
    maxima = jnp.full((row_count,), FLOOR, jnp.float32)
    scores = (
        matmul(queries[:, :nope], key_own.T)
        + matmul(queries[:, nope:], portion[:, nope:shared_end].T)
    ) * score_scale
    key_pos = jnp.arange(key_own.shape[0], dtype=jnp.int32)
    causal = query_pos[:, None] >= key_pos[None, :]
    scores = jnp.where(causal, scores, FLOOR)
    new_max = jnp.maximum(maxima, jnp.max(scores, axis=1))
    weights = jnp.where(causal, jnp.exp(scores - new_max[:, None]), 0.0)
    attended = matmul(weights, portion[:, shared_end:]) / jnp.sum(weights, axis=1)[:, None]
    return lax.psum_scatter(matmul(attended, w_out), "head", scatter_dimension=0, tiled=True)


def solution(mesh):
    placed = (
        P(("ctx", "head"), None),
        P(None, "head"),
        P(),
        P(),
        P(None, "head"),
        P(None, "head"),
        P("head", None),
    )
    return jax.shard_map(
        on_device, mesh=mesh, in_specs=placed, out_specs=P(("ctx", "head"), None), check_vma=False
    )
```

profile of v0, /device:TPU:24, one launch (start us, length us, event | category | flops | bytes accessed | tf_op | source)
XLA Modules:
  0.0 133.6 jit_solution(8996285080578068677)
XLA Ops:
  6.5 0.0 copy-start
  6.5 0.0 all-gather.3.cloned.1.call-start
  6.5 0.7 all-gather.3.cloned.1.call-update
  7.3 0.0 copy-start.4
  7.3 0.0 all-gather.5.cloned.1.call-start
  7.3 7.1 %fusion.19 = f32[32,576]{1,0:T(8,128)S(1)} fusion(f32[32,2304]{1,0:T(8,128)} %param.7, f32[2304,576]{0,1:T(8,128)} %param.9), kind=kOutput, calls=%fused_computation.30 | convolution fusion | flops 509607936 | bytes 5677056 | tf_op jit(solution)/shard_map/dot_general | solution.py:12
  14.5 0.0 copy-start.2
  14.5 0.0 copy-start.3
  14.5 0.1 multiply_reduce_fusion
  14.6 0.0 copy-done.4
  14.6 0.1 multiply_multiply_fusion
  14.7 12.0 %all_gather.10 = f32[256,576]{1,0:T(8,128)S(1)} all-gather(f32[32,576]{1,0:T(8,128)S(1)} %pad_maximum_fusion.1), channel_id=1, replica_groups=mesh['ctx'=4,'head'=8] {'head'}, dimensions={0}, use_global_device_ids=true | all-gather | bytes 663552 | tf_op jit(solution)/shard_map/all_gather | solution.py:24
  26.7 0.1 copy.8
  26.8 0.0 copy-done.2
  26.8 0.6 fusion.8
  27.4 0.0 copy-done.3
  27.4 0.6 fusion.10
  28.0 0.7 pad_maximum_fusion
  28.7 0.0 all-gather.5.cloned.1.call-update
  28.8 0.2 reduce-scatter.2.cloned.1.call-start
  29.0 12.0 %all-gather.3.cloned.1.call-done = f32[256,2304]{1,0:T(8,128)} async-done(((f32[32,2304]{1,0:T(8,128)}), f32[256,2304]{1,0:T(8,128)}) %all-gather.3.cloned.1.call-update) | async-done | bytes 2359312 | tf_op jit(solution)/shard_map/all_gather | solution.py:25
  41.0 0.0 copy-done
  41.0 4.1 %fusion.18 = f32[256,192]{0,1:T(8,128)S(1)} fusion(f32[256,2304]{1,0:T(8,128)} %all-gather.3.cloned.1.call-done, f32[2304,192]{0,1:T(8,128)S(1)} %copy-done), kind=kOutput, calls=%fused_computation.29 | convolution fusion | flops 1358954496 | bytes 4325376 | tf_op jit(solution)/shard_map/dot_general | solution.py:12
  45.1 28.2 %all-gather.5.cloned.1.call-done = f32[1024,320]{0,1:T(8,128)} async-done(((f32[256,320]{0,1:T(8,128)}), f32[1024,320]{0,1:T(8,128)}) %all-gather.5.cloned.1.call-update) | async-done | bytes 1310736 | tf_op jit(solution)/shard_map/all_gather | solution.py:35
  73.3 2.0 %fusion.12 = f32[256,1024]{1,0:T(8,128)S(1)} fusion(f32[1024,320]{0,1:T(8,128)} %all-gather.5.cloned.1.call-done, f32[256,192]{0,1:T(8,128)S(1)} %fusion.18), kind=kOutput, calls=%fused_computation.17 | convolution fusion | flops 201326592 | bytes 1376256 | tf_op jit(solution)/shard_map/dot_general | solution.py:12
  75.3 2.3 %fusion.17 = (f32[256]{0:T(256)S(1)}, f32[256,1024]{1,0:T(8,128)S(1)}) fusion(f32[256,1024]{1,0:T(8,128)S(1)} %fusion.12, f32[1024,320]{0,1:T(8,128)} %all-gather.5.cloned.1.call-done, f32[256,192]{0,1:T(8,128)S(1)} %fusion.18, s32[256]{0:T(256)S(1)} %iota_add_fusion), kind=kOutput, calls=%fused_computation.28 | convolution fusion | flops 403963648 | bytes 2754560 | tf_op jit(solution)/shard_map/dot_general | solution.py:12
  77.6 0.0 copy-start.1
  77.6 0.4 fusion.2
  78.0 2.2 %convolution_divide_fusion = f32[256,128]{1,0:T(8,128)S(1)} fusion(f32[256,1024]{1,0:T(8,128)S(1)} %get-tuple-element.6, f32[1024,320]{0,1:T(8,128)} %all-gather.5.cloned.1.call-done, f32[256]{0:T(256)S(1)} %broadcast_maximum_fusion, s32[256]{0:T(256)S(1)} %iota_add_fusion, f32[256]{0:T(256)S(1)} %fusion.2), kind=kOutput, calls=%fused_computation.3 | convolution fusion | flops 403472384 | bytes 1707008 | tf_op jit(solution)/shard_map/dot_general | solution.py:12
  80.2 0.0 copy-done.1
  80.2 3.4 %fusion.20 = f32[256,2304]{1,0:T(8,128)} fusion(f32[256,128]{1,0:T(8,128)S(1)} %convolution_divide_fusion, f32[128,2304]{1,0:T(8,128)S(1)} %copy-done.1), kind=kOutput, calls=%fused_computation.31 | convolution fusion | flops 905969664 | bytes 3670016 | tf_op jit(solution)/shard_map/dot_general | solution.py:12
  83.7 0.0 reduce-scatter.2.cloned.1.call-update
  83.7 43.4 %reduce-scatter.2.cloned.1.call-done = f32[32,2304]{1,0:T(8,128)} async-done(((f32[256,2304]{1,0:T(8,128)}), f32[32,2304]{1,0:T(8,128)}) %reduce-scatter.2.cloned.1.call-update) | async-done | bytes 294928 | tf_op jit(solution)/shard_map/reduce_scatter | solution.py:48
  (6 shorter events, 0.0 us)
Async XLA Ops:
  6.5 34.5 %copy-start = (f32[2304,192]{0,1:T(8,128)S(1)}, f32[2304,192]{0,1:T(8,128)}, u32[]{:S(2)}) copy-start(f32[2304,192]{0,1:T(8,128)} %param.8) | copy-start | bytes 5308420
  6.5 34.5 %all-gather.3.cloned.1.call-start = ((), (), s32[]{:S(2)}) async-start(), calls=%async_computation.1 | async-start | bytes 2654208 | tf_op jit(solution)/shard_map/all_gather | solution.py:25
  7.3 7.4 %copy-start.4 = (f32[512]{0:T(512)S(1)}, f32[512]{0:T(512)}, u32[]{:S(2)}) copy-start(f32[512]{0:T(512)} %param.10) | copy-start | bytes 6148
  7.3 66.0 %all-gather.5.cloned.1.call-start = ((), (), s32[]{:S(2)}) async-start(), calls=%async_computation.2 | async-start | bytes 1638400 | tf_op jit(solution)/shard_map/all_gather | solution.py:35
  14.5 12.3 %copy-start.2 = (f32[512,128]{1,0:T(8,128)S(1)}, f32[512,128]{1,0:T(8,128)}, u32[]{:S(2)}) copy-start(f32[512,128]{1,0:T(8,128)} %param.12) | copy-start | bytes 786436
  14.5 12.9 %copy-start.3 = (f32[512,128]{1,0:T(8,128)S(1)}, f32[512,128]{1,0:T(8,128)}, u32[]{:S(2)}) copy-start(f32[512,128]{1,0:T(8,128)} %param.11) | copy-start | bytes 786436
  28.8 98.3 %reduce-scatter.2.cloned.1.call-start = ((), (), s32[]{:S(2)}) async-start(), calls=%async_computation.3 | async-start | bytes 2654208 | tf_op jit(solution)/shard_map/reduce_scatter | solution.py:48
  77.6 2.6 %copy-start.1 = (f32[128,2304]{1,0:T(8,128)S(1)}, f32[128,2304]{1,0:T(8,128)}, u32[]{:S(2)}) copy-start(f32[128,2304]{1,0:T(8,128)} %param.13) | copy-start | bytes 3538948
Sparse Core Ops, SparseCore 0:
  9.2 31.7 all-gather.2
  42.6 30.6 all-gather.4
  83.8 43.2 reduce-scatter.1
where the time goes:
time: 136 us; the launch traced here: 134 us
  waiting for transfers between devices  84.3 us (62%)
  matrix products  22.4 us (16%)
  between operations  13.3 us (10%)
  blocking collectives  12 us (9%)
    reduce_scatter x1, waiting for transfers between devices, on_device(): lax.psum_scatter(matmul(attended, w_out), 'head', scatter_dimension=0, ti...  43.4 us
    all_gather x1, waiting for transfers between devices, on_device(): portion = lax.all_gather(projected, 'ctx', axis=0, tiled=True)  28.2 us
    dot_general x8, matrix products, matmul(): jnp.dot(left, right, precision=EXACT, preferred_element_type=jnp.float32)  22.4 us
    all_gather x1, waiting for transfers between devices, on_device(): lax.all_gather(hidden, 'head', axis=0, tiled=True)  12 us
    all_gather x1, blocking collectives, on_device(): latent_block = lax.all_gather(own_latent, 'head', axis=0, tiled=True)  12 us
  transfers between devices with their start and end apart: 3, of which 3 were waited for; matrix products, arithmetic and copies ran while one was open for 10% of the time, Pallas kernels for 0%

commit v1 on v0

v1 whole, which is shorter than its diff:
```python
import functools

import jax
import jax.numpy as jnp
from jax import lax
from jax.experimental import pallas as pl
from jax.experimental.pallas import tpu as pltpu
from jax.sharding import PartitionSpec as P

EPSILON = 1e-06
FLOOR = -1e30
CORES = 2
MESH = pl.DeviceIdType.MESH
NN = (((1,), (0,)), ((), ()))
NT = (((1,), (1,)), ((), ()))


def halves(value):
    high = value.astype(jnp.bfloat16)
    return high, (value - high.astype(jnp.float32)).astype(jnp.bfloat16)


def product(left, right, dims=NN):
    (lh, ll), (rh, rl) = left, right
    dot = functools.partial(lax.dot_general, dimension_numbers=dims, preferred_element_type=jnp.float32)
    return dot(lh, rh) + (dot(ll, rh) + dot(lh, rl))


def divisor(extent, wish):
    while extent % wish:
        wish //= 2
    return wish


def kernel(
    ctx_n, chips, steps, pieces,
    hidden, w_query, w_down, gain, w_key, w_value, w_out, out,
    hid, wd, wq, gn, wk, wv, wo, lat, qh, ql, top, total, acc, part, landed,
    load_sem, swap_send, swap_recv, hid_send, hid_recv, col_send, col_recv,
    row_send, row_recv, twin_send, twin_recv, sum_send, sum_recv,
):
    rows, width = hidden.shape
    rank = gn.shape[1]
    tail = wd.shape[1] - rank
    nope = wk.shape[2]
    per_core = chips * rows
    block = CORES * per_core
    lanes = lat.shape[1]
    ctx = lax.axis_index("ctx")
    head = lax.axis_index("head")
    chip, core = head // CORES, head % CORES
    twin = chip * CORES + (1 - core)

    def chip_at(offset):
        return lax.rem(chip + offset, chips)

    def local(src, dst, sem):
        return pltpu.make_async_copy(src, dst, load_sem.at[sem])

    def remote(src, dst, send, recv, c, h):
        return pltpu.make_async_remote_copy(
            src_ref=src, dst_ref=dst, send_sem=send, recv_sem=recv,
            device_id={"ctx": c, "head": h}, device_id_type=MESH,
        )

    def at_rows(start, size):
        return pl.ds(pl.multiple_of(start, 8), size)

    my_hid = hid.at[at_rows(chip * rows, rows)]
    depth = width // steps
    loads = [local(hidden, my_hid, 0), local(gain, gn, 1)]
    for s in range(steps):
        loads.append(local(w_down.at[pl.ds(s * depth, depth)], wd.at[pl.ds(s * depth, depth)], 2 + s))
    pairs = [(w_query, wq), (w_key, wk), (w_value, wv), (w_out, wo)]
    own = [local(src, dst.at[core], 2 + steps + i) for i, (src, dst) in enumerate(pairs)]
    for copy in loads:
        copy.start()

    barrier = pltpu.get_barrier_semaphore()
    for o in range(1, chips):
        pl.semaphore_signal(barrier, inc=1, device_id={"ctx": ctx, "head": chip_at(o) * CORES + core}, device_id_type=MESH)
    pl.semaphore_signal(barrier, inc=1, device_id={"ctx": ctx, "head": twin}, device_id_type=MESH)
    for o in range(1, ctx_n):
        pl.semaphore_signal(barrier, inc=1, device_id={"ctx": lax.rem(ctx + o, ctx_n), "head": head}, device_id_type=MESH)
    pl.semaphore_wait(barrier, chips - 1 + 1 + ctx_n - 1)

    def hid_copy(o, k):
        return remote(hidden, hid.at[at_rows(k * rows, rows)], hid_send.at[o], hid_recv.at[k], ctx, chip_at(o) * CORES + core)

    for o in range(1, chips):
        hid_copy(o, chip).start()
    swaps = [remote(src, dst.at[core], swap_send.at[i], swap_recv.at[i], ctx, twin) for i, (src, dst) in enumerate(pairs)]
    for copy in own:
        copy.start()
    for copy in swaps:
        copy.start()

    loads[0].wait()
    loads[1].wait()
    down = jnp.zeros((rows, rank + tail), jnp.float32)
    for s in range(steps):
        loads[2 + s].wait()
        span = pl.ds(s * depth, depth)
        down += product(halves(my_hid[:, span]), halves(wd[span, :]))
    raw = down[:, :rank]
    meansq = jnp.mean(raw * raw, axis=-1, keepdims=True)
    blank = jnp.zeros((rows, lanes - rank - tail), jnp.float32)

    def place(b, p, k):
        return ((b * CORES + p) * chips + k) * rows

    mine = at_rows(place(ctx, core, chip), rows)
    lat[mine, :rank] = raw * lax.rsqrt(meansq + EPSILON) * gn[...]
    lat[mine, rank:] = jnp.concatenate([down[:, rank:], blank], axis=1)

    def col_copy(b):
        spot = lat.at[at_rows(place(b, core, chip), rows)]
        return remote(spot, spot, col_send.at[b], col_recv.at[b], jnp.minimum(ctx + 1, ctx_n - 1), head)

    def row_copy(b, o, k):
        spot = lat.at[at_rows(place(b, core, k), rows)]
        return remote(spot, spot, row_send.at[b, o], row_recv.at[b, k], ctx, chip_at(o) * CORES + core)

    def twin_copy(b, p):
        spot = lat.at[at_rows(place(b, p, 0), per_core)]
        return remote(spot, spot, twin_send.at[b], twin_recv.at[b], ctx, twin)

    def spread(b):
        @pl.when(ctx + 1 < ctx_n)
        def _():
            col_copy(b).start()

        for o in range(1, chips):
            row_copy(b, o, chip).start()

    def gather_rows(b):
        for o in range(1, chips):
            row_copy(b, 0, chip_at(o)).wait_recv()
        twin_copy(b, core).start()

    spread(ctx)
    for d in range(1, ctx_n):
        @pl.when(d <= ctx)
        def _():
            col_copy(ctx - d).wait_recv()
            spread(ctx - d)

    gather_rows(ctx)

    for o in range(1, chips):
        hid_copy(0, chip_at(o)).wait_recv()
    for i in range(2):
        own[i].wait()
        swaps[i].wait()
    scale = wq.shape[2] ** (-0.5)
    pad = jnp.zeros((per_core, lanes - rank - tail), jnp.float32)
    query = [jnp.zeros((per_core, wq.shape[2]), jnp.float32) for _ in range(CORES)]
    for s in range(steps):
        span = pl.ds(s * depth, depth)
        piece = halves(hid[:, span])
        for p in range(CORES):
            query[p] += product(piece, halves(wq[p, span, :]))
    for p in range(CORES):
        wide = product(halves(query[p][:, :nope] * scale), halves(wk[p]), NT)
        span = pl.ds(p * per_core, per_core)
        qh[span, :rank], ql[span, :rank] = halves(wide)
        qh[span, rank:], ql[span, rank:] = halves(jnp.concatenate([query[p][:, nope:] * scale, pad], axis=1))

    def spots(index, parity):
        inner = lax.rem(index, per_core)
        return (lax.div(inner, rows) * CORES + parity) * rows + lax.rem(inner, rows)

    def attend(b, first):
        keys = halves(lat[at_rows(place(b, 0, 0), block), :])
        scores = product((qh[...], ql[...]), keys, NT)
        if first:
            line = lax.broadcasted_iota(jnp.int32, (block, 1), 0)
            column = lax.broadcasted_iota(jnp.int32, (1, block), 1)
            causal = spots(line, core) >= spots(column, lax.div(column, per_core))
            scores = jnp.where(causal, scores, FLOOR)
            peak = jnp.max(scores, axis=1, keepdims=True)
        else:
            peak = jnp.maximum(top[...], jnp.max(scores, axis=1, keepdims=True))
        weights = jnp.exp(scores - peak)
        if first:
            weights = jnp.where(causal, weights, 0.0)
        mixed = product(halves(weights), (keys[0][:, :rank], keys[1][:, :rank]))
        added = jnp.sum(weights, axis=1, keepdims=True)
        if first:
            total[...] = added
            acc[...] = mixed
        else:
            fade = jnp.exp(top[...] - peak)
            total[...] = total[...] * fade + added
            acc[...] = acc[...] * fade + mixed
        top[...] = peak

    twin_copy(ctx, 1 - core).wait_recv()
    attend(ctx, True)
    for d in range(1, ctx_n):
        @pl.when(d <= ctx)
        def _():
            gather_rows(ctx - d)
            twin_copy(ctx - d, 1 - core).wait_recv()
            attend(ctx - d, False)

    for i in range(2, 4):
        own[i].wait()
        swaps[i].wait()
    heads = []
    for p in range(CORES):
        span = pl.ds(p * per_core, per_core)
        heads.append(product(halves(acc[span, :] / total[span, :]), halves(wv[p])))
    attended = halves(jnp.concatenate(heads, axis=1))
    columns = width // pieces

    def sum_copy(t, o, k):
        span = pl.ds(t * columns, columns)
        return remote(
            part.at[at_rows(chip_at(o) * rows, rows), span], landed.at[at_rows(k * rows, rows), span],
            sum_send.at[t, o], sum_recv.at[t, k], ctx, chip_at(o) * CORES + core,
        )

    for t in range(pieces):
        span = pl.ds(t * columns, columns)
        weight = jnp.concatenate([wo[p, :, span] for p in range(CORES)], axis=0)
        part[:, span] = product(attended, halves(weight))
        for o in range(1, chips):
            sum_copy(t, o, chip).start()
    for t in range(pieces):
        span = pl.ds(t * columns, columns)
        result = part[at_rows(chip * rows, rows), span]
        for o in range(1, chips):
            sum_copy(t, 0, chip_at(o)).wait_recv()
            result += landed[at_rows(chip_at(o) * rows, rows), span]
        out[:, span] = result

    for o in range(1, chips):
        hid_copy(o, chip).wait_send()
        for t in range(pieces):
            sum_copy(t, o, chip).wait_send()
    for d in range(ctx_n):
        @pl.when(d <= ctx)
        def _():
            @pl.when(ctx + 1 < ctx_n)
            def _():
                col_copy(ctx - d).wait_send()

            for o in range(1, chips):
                row_copy(ctx - d, o, chip).wait_send()
            twin_copy(ctx - d, core).wait_send()


def on_device(ctx_n, chips, hidden, w_query, w_down, latent_gain, w_key_up, w_value_up, w_out):
    rows, width = hidden.shape
    rank, nope = w_key_up.shape
    vdim = w_value_up.shape[1]
    per_core = chips * rows
    block = CORES * per_core
    lanes = -(-w_down.shape[1] // 128) * 128
    steps = 3 if width % 384 == 0 else 1
    pieces = 3 if width % 384 == 0 else 1
    f32, bf16, dma = jnp.float32, jnp.bfloat16, pltpu.SemaphoreType.DMA
    return pl.pallas_call(
        functools.partial(kernel, ctx_n, chips, steps, pieces),
        out_shape=jax.ShapeDtypeStruct((rows, width), f32),
        in_specs=[pl.BlockSpec(memory_space=pl.ANY)] * 7,
        out_specs=pl.BlockSpec(memory_space=pltpu.VMEM),
        scratch_shapes=[
            pltpu.VMEM((per_core, width), f32),
            pltpu.VMEM(w_down.shape, f32),
            pltpu.VMEM((CORES,) + w_query.shape, f32),
            pltpu.VMEM((1, rank), f32),
            pltpu.VMEM((CORES, rank, nope), f32),
            pltpu.VMEM((CORES, rank, vdim), f32),
            pltpu.VMEM((CORES, vdim, width), f32),
            pltpu.VMEM((ctx_n * block, lanes), f32),
            pltpu.VMEM((block, lanes), bf16),
            pltpu.VMEM((block, lanes), bf16),
            pltpu.VMEM((block, 1), f32),
            pltpu.VMEM((block, 1), f32),
            pltpu.VMEM((block, rank), f32),
            pltpu.VMEM((per_core, width), f32),
            pltpu.VMEM((per_core, width), f32),
            dma((2 + steps + 4,)),
            dma((4,)), dma((4,)),
            dma((chips,)), dma((chips,)),
            dma((ctx_n,)), dma((ctx_n,)),
            dma((ctx_n, chips)), dma((ctx_n, chips)),
            dma((ctx_n,)), dma((ctx_n,)),
            dma((pieces, chips)), dma((pieces, chips)),
        ],
        compiler_params=pltpu.CompilerParams(
            collective_id=0, has_side_effects=True, vmem_limit_bytes=56 * 1024 * 1024
        ),
    )(hidden, w_query, w_down, latent_gain.reshape(1, rank), w_key_up, w_value_up, w_out)


def solution(mesh):
    placed = (
        P(("ctx", "head"), None),
        P(None, "head"),
        P(),
        P(),
        P(None, "head"),
        P(None, "head"),
        P("head", None),
    )
    body = functools.partial(on_device, mesh.shape["ctx"], mesh.shape["head"] // CORES)
    return jax.shard_map(
        body, mesh=mesh, in_specs=placed, out_specs=P(("ctx", "head"), None), check_vma=False
    )
```

time: 136 us -> 62.1 us (0.46); the launches traced: 134 us -> 61.9 us
  waiting for transfers between devices: 84.3 us -> 0 us
  Pallas kernels: 0 us -> 50.9 us
  matrix products: 22.4 us -> 0 us
  between operations: 13.3 us -> 0.01 us
  blocking collectives: 12 us -> 0 us
  local copies, waits for them, and re-layouts: 0.12 us -> 11 us
    pallas_call x0 -> x1, Pallas kernels: none -> 50.9 us  [on_device(): pl.pallas_call(functools.partial(kernel, ctx_n, chips, steps, pieces), ou...]
    reduce_scatter x1 -> x0, waiting for transfers between devices: 43.4 us -> none  [on_device(): lax.psum_scatter(matmul(attended, w_out), 'head', scatter_dimension=0, ti...]
    all_gather x2 -> x0, waiting for transfers between devices: 40.2 us -> none  [the longest x1 28.2 us: on_device(): portion = lax.all_gather(projected, 'ctx', axis=0, tiled=True)]
    dot_general x8 -> x0, matrix products: 22.4 us -> none  [matmul(): jnp.dot(left, right, precision=EXACT, preferred_element_type=jnp.float32)]
    all_gather x1 -> x0, blocking collectives: 12 us -> none  [on_device(): latent_block = lax.all_gather(own_latent, 'head', axis=0, tiled=True)]
    unnamed x10 -> x3, local copies, waits for them, and re-layouts: 0.02 us -> 11 us
  transfers between devices with their start and end apart: 3 -> 0, of which waited for: 3 -> 0; matrix products, arithmetic and copies ran while one was open for 10% -> 0% of each run, Pallas kernels for 0% -> 0%
where the time goes in v1:
time: 62.1 us; the launch traced here: 61.9 us
  Pallas kernels  50.9 us (82%)
  local copies, waits for them, and re-layouts  11 us (18%)
    pallas_call x1, Pallas kernels, on_device(): pl.pallas_call(functools.partial(kernel, ctx_n, chips, steps, pieces), ou...  50.9 us
    unnamed x3, local copies, waits for them, and re-layouts  11 us

profile of v1, /device:TPU:24, one launch (start us, length us, event | category | flops | bytes accessed | tf_op | source)
XLA Modules:
  0.0 61.9 jit_solution(13198617767379462843)
XLA Ops:
  0.0 2.9 %copy.8.w_query = f32[2304,192]{1,0:T(8,128)} copy(f32[2304,192]{0,1:T(8,128)} %param.8) | data formatting | bytes 3538944 | tf_op args[1]
  2.9 6.4 %copy.9.w_down = f32[2304,576]{1,0:T(8,128)} copy(f32[2304,576]{0,1:T(8,128)} %param.9) | data formatting | bytes 10616832 | tf_op args[2]
  9.3 50.9 %shard_map.73 = f32[32,2304]{1,0:T(8,128)} custom-call(f32[32,2304]{1,0:T(8,128)} %hidden.1, f32[2304,192]{1,0:T(8,128)} %copy.8.w_query, f32[2304,576]{1,0:T(8,128)} %copy.9.w_down, f32[1,512]{1,0:T(1,128)} %bitcast.1, f32[512,128]{1,0:T(8,128)} %w_key.1, f32[512,128]{1,0:T(8,128)} %w_value.1, f32[128,2304]{1,0:T(8,128)} %w_out.1), custom_call_target="tpu_custom_call" | custom-call | tf_op jit(solution)/shard_map/pallas_call | solution.py:264
  60.2 1.7 %copy.11 = f32[32,2304]{1,0:T(8,128)} copy(f32[32,2304]{1,0:T(8,128)} %shard_map.73) | data formatting | bytes 589824

commit v2 on v1

--- a/solution.py
+++ b/solution.py
@@ -26,22 +26,17 @@
     return dot(lh, rh) + (dot(ll, rh) + dot(lh, rl))
 
 
-def divisor(extent, wish):
-    while extent % wish:
-        wish //= 2
-    return wish
-
-
 def kernel(
-    ctx_n, chips, steps, pieces,
+    ctx_n, chips, square, steps, pieces,
     hidden, w_query, w_down, gain, w_key, w_value, w_out, out,
     hid, wd, wq, gn, wk, wv, wo, lat, qh, ql, top, total, acc, part, landed,
     load_sem, swap_send, swap_recv, hid_send, hid_recv, col_send, col_recv,
     row_send, row_recv, twin_send, twin_recv, sum_send, sum_recv,
 ):
     rows, width = hidden.shape
+    parts = 2 if square else 1
     rank = gn.shape[1]
-    tail = wd.shape[1] - rank
+    tail = wd.shape[0] - rank
     nope = wk.shape[2]
     per_core = chips * rows
     block = CORES * per_core
@@ -54,6 +49,14 @@
     def chip_at(offset):
         return lax.rem(chip + offset, chips)
 
+    def to(o):
+        if not square:
+            return chip_at(o)
+        return [chip, chip + 1 - 2 * lax.rem(chip, 2), lax.rem(chip + 2, 4), 3 - chip][o]
+
+    def origin(o):
+        return to(o) if square else chip_at(chips - o)
+
     def local(src, dst, sem):
         return pltpu.make_async_copy(src, dst, load_sem.at[sem])
 
@@ -70,7 +73,8 @@
     depth = width // steps
     loads = [local(hidden, my_hid, 0), local(gain, gn, 1)]
     for s in range(steps):
-        loads.append(local(w_down.at[pl.ds(s * depth, depth)], wd.at[pl.ds(s * depth, depth)], 2 + s))
+        span = pl.ds(s * depth, depth)
+        loads.append(local(w_down.at[:, span], wd.at[:, span], 2 + s))
     pairs = [(w_query, wq), (w_key, wk), (w_value, wv), (w_out, wo)]
     own = [local(src, dst.at[core], 2 + steps + i) for i, (src, dst) in enumerate(pairs)]
     for copy in loads:
@@ -84,11 +88,56 @@
         pl.semaphore_signal(barrier, inc=1, device_id={"ctx": lax.rem(ctx + o, ctx_n), "head": head}, device_id_type=MESH)
     pl.semaphore_wait(barrier, chips - 1 + 1 + ctx_n - 1)
 
-    def hid_copy(o, k):
-        return remote(hidden, hid.at[at_rows(k * rows, rows)], hid_send.at[o], hid_recv.at[k], ctx, chip_at(o) * CORES + core)
-
-    for o in range(1, chips):
-        hid_copy(o, chip).start()
+    def share(source, spot, send, recv):
+        def start_of(o, h):
+            target = to(o)
+            return remote(source(h), spot(chip, h), send(o, h), recv(o, h), ctx, target * CORES + core)
+
+        def seen(o, h):
+            place_of = spot(origin(o), h)
+            return remote(place_of, place_of, send(o, h), recv(o, h), ctx, twin)
+
+        def passed(h):
+            place_of = spot(to(1 + h), h)
+            return remote(place_of, place_of, send(3, h), recv(3, h), ctx, to(2 - h) * CORES + core)
+
+        direct = [(1, 0), (2, 1), (1, 1), (2, 0)] if square else [(o, 0) for o in range(1, chips)]
+
+        def start():
+            for o, h in direct:
+                start_of(o, h).start()
+
+        def relay():
+            if square:
+                for h in range(2):
+                    seen(1 + h, h).wait_recv()
+                    passed(h).start()
+
+        def finish():
+            for o, h in [(1, 1), (2, 0), (3, 0), (3, 1)] if square else direct:
+                seen(o, h).wait_recv()
+
+        def drain():
+            for o, h in direct:
+                start_of(o, h).wait_send()
+            if square:
+                for h in range(2):
+                    passed(h).wait_send()
+
+        return start, relay, finish, drain
+
+    half = width // parts
+
+    def hid_half(h):
+        return pl.ds(h * half, half)
+
+    hid_start, hid_relay, hid_finish, hid_drain = share(
+        lambda h: hidden.at[:, hid_half(h)],
+        lambda k, h: hid.at[at_rows(k * rows, rows), hid_half(h)],
+        lambda o, h: hid_send.at[o, h],
+        lambda o, h: hid_recv.at[o, h],
+    )
+    hid_start()
     swaps = [remote(src, dst.at[core], swap_send.at[i], swap_recv.at[i], ctx, twin) for i, (src, dst) in enumerate(pairs)]
     for copy in own:
         copy.start()
@@ -101,7 +150,7 @@
     for s in range(steps):
         loads[2 + s].wait()
         span = pl.ds(s * depth, depth)
-        down += product(halves(my_hid[:, span]), halves(wd[span, :]))
+        down += product(halves(my_hid[:, span]), halves(wd[:, span]), NT)
     raw = down[:, :rank]
     meansq = jnp.mean(raw * raw, axis=-1, keepdims=True)
     blank = jnp.zeros((rows, lanes - rank - tail), jnp.float32)
@@ -117,9 +166,13 @@
         spot = lat.at[at_rows(place(b, core, chip), rows)]
         return remote(spot, spot, col_send.at[b], col_recv.at[b], jnp.minimum(ctx + 1, ctx_n - 1), head)
 
-    def row_copy(b, o, k):
-        spot = lat.at[at_rows(place(b, core, k), rows)]
-        return remote(spot, spot, row_send.at[b, o], row_recv.at[b, k], ctx, chip_at(o) * CORES + core)
+    def latents(b):
+        def spot(k, h):
+            return lat.at[at_rows(place(b, core, k) + h * (rows // parts), rows // parts)]
+
+        return share(
+            lambda h: spot(chip, h), spot, lambda o, h: row_send.at[b, o, h], lambda o, h: row_recv.at[b, o, h]
+        )
 
     def twin_copy(b, p):
         spot = lat.at[at_rows(place(b, p, 0), per_core)]
@@ -130,36 +183,34 @@
         def _():
             col_copy(b).start()
 
-        for o in range(1, chips):
-            row_copy(b, o, chip).start()
+        latents(b)[0]()
 
     def gather_rows(b):
-        for o in range(1, chips):
-            row_copy(b, 0, chip_at(o)).wait_recv()
+        latents(b)[2]()
         twin_copy(b, core).start()
 
     spread(ctx)
+    hid_relay()
     for d in range(1, ctx_n):
         @pl.when(d <= ctx)
         def _():
             col_copy(ctx - d).wait_recv()
             spread(ctx - d)
 
-    gather_rows(ctx)
-
-    for o in range(1, chips):
-        hid_copy(0, chip_at(o)).wait_recv()
+    latents(ctx)[1]()
+
+    hid_finish()
     for i in range(2):
         own[i].wait()
         swaps[i].wait()
-    scale = wq.shape[2] ** (-0.5)
+    scale = wq.shape[1] ** (-0.5)
     pad = jnp.zeros((per_core, lanes - rank - tail), jnp.float32)
-    query = [jnp.zeros((per_core, wq.shape[2]), jnp.float32) for _ in range(CORES)]
+    query = [jnp.zeros((per_core, wq.shape[1]), jnp.float32) for _ in range(CORES)]
     for s in range(steps):
         span = pl.ds(s * depth, depth)
         piece = halves(hid[:, span])
         for p in range(CORES):
-            query[p] += product(piece, halves(wq[p, span, :]))
+            query[p] += product(piece, halves(wq[p, :, span]), NT)
     for p in range(CORES):
         wide = product(halves(query[p][:, :nope] * scale), halves(wk[p]), NT)
         span = pl.ds(p * per_core, per_core)
@@ -195,11 +246,20 @@
             acc[...] = acc[...] * fade + mixed
         top[...] = peak
 
+    def relay_at(d):
+        if d < ctx_n:
+            @pl.when(d <= ctx)
+            def _():
+                latents(ctx - d)[1]()
+
+    relay_at(1)
+    gather_rows(ctx)
     twin_copy(ctx, 1 - core).wait_recv()
     attend(ctx, True)
     for d in range(1, ctx_n):
         @pl.when(d <= ctx)
         def _():
+            relay_at(d + 1)
             gather_rows(ctx - d)
             twin_copy(ctx - d, 1 - core).wait_recv()
             attend(ctx - d, False)
@@ -214,31 +274,58 @@
     attended = halves(jnp.concatenate(heads, axis=1))
     columns = width // pieces
 
-    def sum_copy(t, o, k):
-        span = pl.ds(t * columns, columns)
-        return remote(
-            part.at[at_rows(chip_at(o) * rows, rows), span], landed.at[at_rows(k * rows, rows), span],
-            sum_send.at[t, o], sum_recv.at[t, k], ctx, chip_at(o) * CORES + core,
-        )
-
+    def cut(ref, k, t):
+        return ref.at[at_rows(k * rows, rows), pl.ds(t * columns, columns)]
+
+    def axes_of(t):
+        return (1, 2) if t % 2 == 0 else (2, 1)
+
+    def sum_copy(t, j):
+        if not square:
+            return remote(
+                cut(part, chip_at(j), t), cut(landed, chip, t), sum_send.at[t, j], sum_recv.at[t, j],
+                ctx, chip_at(j) * CORES + core,
+            )
+        first, second = axes_of(t)
+        src = [to(3), to(first), to(second)][j]
+        dst = [to(3), to(first), to(3)][j]
+        target = [to(first), to(first), to(second)][j]
+        return remote(cut(part, src, t), cut(landed, dst, t), sum_send.at[t, j], sum_recv.at[t, j], ctx, target * CORES + core)
+
+    def second_stage(t):
+        sum_copy(t, 0).wait_recv()
+        keep = to(axes_of(t)[1])
+        cut(part, keep, t)[...] = cut(part, keep, t)[...] + cut(landed, keep, t)[...]
+        sum_copy(t, 2).start()
+
+    kinds = (0, 1) if square else tuple(range(1, chips))
     for t in range(pieces):
         span = pl.ds(t * columns, columns)
         weight = jnp.concatenate([wo[p, :, span] for p in range(CORES)], axis=0)
         part[:, span] = product(attended, halves(weight))
-        for o in range(1, chips):
-            sum_copy(t, o, chip).start()
+        for j in kinds:
+            sum_copy(t, j).start()
+        if square and t >= 2:
+            second_stage(t - 2)
+    if square:
+        for t in range(max(pieces - 2, 0), pieces):
+            second_stage(t)
     for t in range(pieces):
-        span = pl.ds(t * columns, columns)
-        result = part[at_rows(chip * rows, rows), span]
-        for o in range(1, chips):
-            sum_copy(t, 0, chip_at(o)).wait_recv()
-            result += landed[at_rows(chip_at(o) * rows, rows), span]
-        out[:, span] = result
-
-    for o in range(1, chips):
-        hid_copy(o, chip).wait_send()
-        for t in range(pieces):
-            sum_copy(t, o, chip).wait_send()
+        result = cut(part, chip, t)[...]
+        if square:
+            for j in (1, 2):
+                sum_copy(t, j).wait_recv()
+            result += cut(landed, chip, t)[...] + cut(landed, to(axes_of(t)[0]), t)[...]
+        else:
+            for j in kinds:
+                sum_copy(t, j).wait_recv()
+                result += cut(landed, origin(j), t)[...]
+        out[:, pl.ds(t * columns, columns)] = result
+
+    hid_drain()
+    for t in range(pieces):
+        for j in kinds + ((2,) if square else ()):
+            sum_copy(t, j).wait_send()
     for d in range(ctx_n):
         @pl.when(d <= ctx)
         def _():
@@ -246,8 +333,7 @@
             def _():
                 col_copy(ctx - d).wait_send()
 
-            for o in range(1, chips):
-                row_copy(ctx - d, o, chip).wait_send()
+            latents(ctx - d)[3]()
             twin_copy(ctx - d, core).wait_send()
 
 
@@ -259,17 +345,18 @@
     block = CORES * per_core
     lanes = -(-w_down.shape[1] // 128) * 128
     steps = 3 if width % 384 == 0 else 1
-    pieces = 3 if width % 384 == 0 else 1
+    square = chips == 4 and rows % 16 == 0 and width % 256 == 0
+    pieces = 6 if width % 768 == 0 else 2
     f32, bf16, dma = jnp.float32, jnp.bfloat16, pltpu.SemaphoreType.DMA
     return pl.pallas_call(
-        functools.partial(kernel, ctx_n, chips, steps, pieces),
+        functools.partial(kernel, ctx_n, chips, square, steps, pieces),
         out_shape=jax.ShapeDtypeStruct((rows, width), f32),
-        in_specs=[pl.BlockSpec(memory_space=pl.ANY)] * 7,
+        in_specs=[pl.BlockSpec(memory_space=pltpu.HBM)] * 7,
         out_specs=pl.BlockSpec(memory_space=pltpu.VMEM),
         scratch_shapes=[
             pltpu.VMEM((per_core, width), f32),
-            pltpu.VMEM(w_down.shape, f32),
-            pltpu.VMEM((CORES,) + w_query.shape, f32),
+            pltpu.VMEM(w_down.shape[::-1], f32),
+            pltpu.VMEM((CORES,) + w_query.shape[::-1], f32),
             pltpu.VMEM((1, rank), f32),
             pltpu.VMEM((CORES, rank, nope), f32),
             pltpu.VMEM((CORES, rank, vdim), f32),
@@ -284,16 +371,16 @@
             pltpu.VMEM((per_core, width), f32),
             dma((2 + steps + 4,)),
             dma((4,)), dma((4,)),
-            dma((chips,)), dma((chips,)),
+            dma((chips, 2)), dma((chips, 2)),
             dma((ctx_n,)), dma((ctx_n,)),
-            dma((ctx_n, chips)), dma((ctx_n, chips)),
+            dma((ctx_n, chips, 2)), dma((ctx_n, chips, 2)),
             dma((ctx_n,)), dma((ctx_n,)),
             dma((pieces, chips)), dma((pieces, chips)),
         ],
         compiler_params=pltpu.CompilerParams(
-            collective_id=0, has_side_effects=True, vmem_limit_bytes=56 * 1024 * 1024
+            collective_id=0, has_side_effects=True, vmem_limit_bytes=60 * 1024 * 1024
         ),
-    )(hidden, w_query, w_down, latent_gain.reshape(1, rank), w_key_up, w_value_up, w_out)
+    )(hidden, w_query.T, w_down.T, latent_gain.reshape(1, rank), w_key_up, w_value_up, w_out)
 
 
 def solution(mesh):

time: 62.1 us -> 51.7 us (0.83)
  local copies, waits for them, and re-layouts: 11 us -> 1.69 us
  Pallas kernels: 50.9 us -> 49.9 us
    unnamed x3 -> x1, local copies, waits for them, and re-layouts: 11 us -> 1.69 us
    pallas_call x1, Pallas kernels: 50.9 us -> 49.9 us  [on_device(): pl.pallas_call(functools.partial(kernel, ctx_n, chips, square, steps, pie...]
where the time goes in v2:
time: 51.7 us; the launch traced here: 51.6 us
  Pallas kernels  49.9 us (97%)
  local copies, waits for them, and re-layouts  1.69 us (3%)
    pallas_call x1, Pallas kernels, on_device(): pl.pallas_call(functools.partial(kernel, ctx_n, chips, square, steps, pie...  49.9 us
    unnamed x1, local copies, waits for them, and re-layouts  1.69 us

profile of v2, /device:TPU:24, one launch (start us, length us, event | category | flops | bytes accessed | tf_op | source)
XLA Modules:
  0.0 51.6 jit_solution(17369497597061734305)
XLA Ops:
  0.0 49.9 %shard_map.73 = f32[32,2304]{1,0:T(8,128)} custom-call(f32[32,2304]{1,0:T(8,128)} %hidden.1, f32[192,2304]{1,0:T(8,128)} %bitcast.4, f32[576,2304]{1,0:T(8,128)} %bitcast.3, f32[1,512]{1,0:T(1,128)} %bitcast.5, f32[512,128]{1,0:T(8,128)} %w_key.1, f32[512,128]{1,0:T(8,128)} %w_value.1, f32[128,2304]{1,0:T(8,128)} %w_out.1), custom_call_target="tpu_custom_call" | custom-call | tf_op jit(solution)/shard_map/pallas_call | solution.py:351
  49.9 1.7 %copy.9 = f32[32,2304]{1,0:T(8,128)} copy(f32[32,2304]{1,0:T(8,128)} %shard_map.73) | data formatting | bytes 589824
